TPU v7x, 256 devices: a whole 4x4x8 slice. The times are simulated.
256 devices in a mesh: pole: 4 (over y), row: 8 (over z), col: 8 (over x, core).
Axes of the slice: x: 4, y: 4, z: 8, core: 2. Of those that a mesh axis runs over, the one named last changes fastest.
Arguments:
- root_inverse: float32 [8, 1024, 1024], P('pole', ('row', 'col')), may hold values from -100 to 100
- node_factor: float32 [8, 8, 1024, 512], P('pole', 'row', None, 'col'), may hold values from -0.1875 to 0.1875
- node_inverse: float32 [8, 8, 512, 512], P('pole', 'row'), may hold values from -100 to 100
- leaf_root_factor: float32 [8, 64, 1024, 256], P('pole', ('row', 'col')), may hold values from -0.1875 to 0.1875
- leaf_node_factor: float32 [8, 64, 512, 256], P('pole', ('row', 'col')), may hold values from -0.25 to 0.25
- leaf_inverse: float32 [8, 64, 256, 256], P('pole', ('row', 'col')), may hold values from -100 to 100
- leaf_pattern: int32 [64, 8], P(('row', 'col')), may hold values 0 or 1
- pole_weight: float32 [8], P('pole'), may hold values from 0.1 to 1
Outputs:
- root_block: float32 [1024, 1024], P(('row', 'col'))
- node_offdiag: float32 [8, 1024, 512], P('row', None, 'col')
- node_diag: float32 [8, 512, 512], P('row', 'col')
- leaf_root: float32 [64, 1024, 256], P(('row', 'col'))
- leaf_node: float32 [64, 512, 256], P(('row', 'col'))
- leaf_diag: float32 [64, 256, 256], P(('row', 'col'))
All inputs are finite; a program needn't handle non-finite values. No bound on the sum of `leaf_pattern` on one device may be relied on, other than what follows from the above.
Results may differ from a plain program's by a relative error of at most 0.0001.
Values sent between devices are 32-bit elements; how exact they have to be, the bound alone decides.
A program may use at most 64 MiB of HBM per device.

v0:
```python
import jax
import jax.numpy as jnp
from jax import lax
from jax.sharding import PartitionSpec as P

highest = lax.Precision.HIGHEST


def product(left, right):
    return jnp.matmul(left, right, precision=highest)


def weighted(weights, values):
    return jnp.sum(weights[:, None, None] * values, axis=0)


def shards(
    root_inverse,
    node_factor,
    node_inverse,
    leaf_root_factor,
    leaf_node_factor,
    leaf_inverse,
    leaf_pattern,
    pole_weight,
):
    node_cols = node_factor[:, 0]
    node_inv = node_inverse[:, 0]
    node_leaf = leaf_node_factor[:, 0]
    leaf_inv = leaf_inverse[:, 0]
    block_rows = leaf_root_factor.shape[2] // leaf_pattern.shape[1]
    row_mask = jnp.repeat(leaf_pattern[0].astype(jnp.float32), block_rows)
    root_leaf = leaf_root_factor[:, 0] * row_mask[None, :, None]
    width = node_cols.shape[2]
    joined = jnp.concatenate([node_cols, root_leaf], axis=2)
    products = product(lax.all_gather(root_inverse, ("row", "col"), axis=1, tiled=True), joined)
    offdiag = -products[:, :, :width]
    root_times = products[:, :, width:]
    col_index = lax.axis_index("col")
    own_rows = lax.dynamic_slice_in_dim(node_inv, col_index * width, width, 1)
    factor_t = jnp.swapaxes(node_cols, 1, 2)
    piece = lax.all_gather(offdiag, "col", axis=2, tiled=True)
    root_sum = root_times
    root_sum = root_sum + product(piece, node_leaf)
    node_part = product(jnp.swapaxes(piece, 1, 2), root_leaf)
    cross = product(factor_t, piece)
    root_sum, node_part, cross = (root_sum, node_part, cross)
    diag_rows = own_rows - cross
    diag_times = product(lax.all_gather(diag_rows, "col", axis=1, tiled=True), node_leaf)
    upper_levels = (
        weighted(pole_weight, root_inverse),
        weighted(pole_weight, offdiag)[None],
        weighted(pole_weight, diag_rows)[None],
    )
    middle_part = node_part + diag_times
    lower_part = (
        leaf_inv
        + product(jnp.swapaxes(root_leaf, 1, 2), root_sum)
        + product(jnp.swapaxes(node_leaf, 1, 2), middle_part)
    )
    leaf_levels = (
        weighted(pole_weight, -root_sum)[None],
        weighted(pole_weight, -middle_part)[None],
        weighted(pole_weight, lower_part)[None],
    )
    totals = lax.psum(
        (
            upper_levels[0],
            upper_levels[1],
            upper_levels[2],
            leaf_levels[0],
            leaf_levels[1],
            leaf_levels[2],
        ),
        "pole",
    )
    return (totals[0], totals[1], totals[2], totals[3], totals[4], totals[5])


def solution(mesh):
    return jax.shard_map(
        shards,
        mesh=mesh,
        in_specs=(
            P("pole", ("row", "col"), None),
            P("pole", "row", None, "col"),
            P("pole", "row", None, None),
            P("pole", ("row", "col"), None, None),
            P("pole", ("row", "col"), None, None),
            P("pole", ("row", "col"), None, None),
            P(("row", "col"), None),
            P("pole"),
        ),
        out_specs=(
            P(("row", "col"), None),
            P("row", None, "col"),
            P("row", "col", None),
            P(("row", "col"), None, None),
            P(("row", "col"), None, None),
            P(("row", "col"), None, None),
        ),
        check_vma=False,
    )
```

profile of v0, /device:TPU:1, one launch (start us, length us, event | category | flops | bytes accessed | tf_op | source)
XLA Modules:
  0.0 272.0 jit_solution(6661913665170530114)
XLA Ops:
  7.2 0.7 all-gather.4.cloned.1.call-update
  8.0 2.9 %copy.20 = f32[2,1,1024,256]{2,3,0,1:T(8,128)} copy(f32[2,1,1024,256]{3,2,1,0:T(8,128)} %param.11) | data formatting | bytes 4194304 | tf_op args[3]
  11.0 1.8 bitcast_multiply_fusion
  12.8 85.2 %all-gather.4.cloned.1.call-done = f32[2,1024,1024]{2,1,0:T(8,128)} async-done(((f32[2,16,1024]{2,1,0:T(8,128)}), f32[2,1024,1024]{2,1,0:T(8,128)}) %all-gather.4.cloned.1.call-update) | async-done | bytes 8388624 | tf_op jit(solution)/shard_map/all_gather | solution.py:36
  98.0 11.3 %fusion.4 = f32[2,1024,320]{1,2,0:T(8,128)S(1)} fusion(f32[2,1024,1024]{2,1,0:T(8,128)} %all-gather.4.cloned.1.call-done, f32[2,1024,256]{1,2,0:T(8,128)S(1)} %bitcast_multiply_fusion, f32[2,1024,64]{1,2,0:T(8,128)} %bitcast.54), kind=kOutput, calls=%fused_computation.7 | convolution fusion | flops 8053719040 | bytes 13631488 | tf_op jit(solution)/shard_map/dot_general | solution.py:10
  109.4 1.5 copy-done.2
  110.9 1.6 slice_negate_fusion
  112.5 31.9 %all-gather.6.cloned.1.call-done = f32[2,1024,512]{1,2,0:T(8,128)} async-done(((f32[2,1024,64]{1,2,0:T(8,128)}), f32[2,1024,512]{1,2,0:T(8,128)}) %all-gather.6.cloned.1.call-update) | async-done | bytes 4194320 | tf_op jit(solution)/shard_map/all_gather | solution.py:42
  144.5 7.9 %multiply_reduce_fusion.3 = (f32[64,512]{1,0:T(8,128)}, f32[2,64,512]{2,1,0:T(8,128)}) fusion(f32[2]{0:T(128)S(1)} %copy-done.11, f32[2,1024,512]{1,2,0:T(8,128)} %all-gather.6.cloned.1.call-done, f32[2,1,1024,64]{2,3,1,0:T(8,128)} %param.9, f32[2,1,512,512]{3,2,1,0:T(8,128)} %param.10, s32[]{:T(128)S(6)} %select_n.3), kind=kOutput, calls=%fused_computation.23 | convolution fusion | flops 805470208 | bytes 5373964 | tf_op jit(solution)/shard_map/dot_general | solution.py:10
  152.4 0.2 all-reduce.3.cloned.1.call-start
  152.6 0.7 multiply_reduce_fusion.4
  153.3 8.0 %multiply_reduce_fusion = (f32[1024,256]{0,1:T(8,128)}, f32[2,1024,256]{1,2,0:T(8,128)S(1)}) fusion(f32[2]{0:T(128)S(1)} %copy-done.11, f32[2,1024,512]{1,2,0:T(8,128)} %all-gather.6.cloned.1.call-done, f32[2,1,512,256]{3,2,1,0:T(8,128)S(1)} %copy-done, f32[2,1024,320]{1,2,0:T(8,128)} %copy-done.2), kind=kOutput, calls=%fused_computation.6 | convolution fusion | flops 3223060480 | bytes 10485768 | tf_op jit(solution)/shard_map/dot_general | solution.py:10
  161.3 2.9 %convolution_add_fusion.1 = f32[2,256,256]{2,1,0:T(8,128)} fusion(f32[2,1024,256]{1,2,0:T(8,128)S(1)} %bitcast_multiply_fusion, f32[2,1024,256]{1,2,0:T(8,128)S(1)} %get-tuple-element.23, f32[2,1,256,256]{3,2,1,0:T(8,128)S(1)} %copy-done.4), kind=kOutput, calls=%fused_computation.11 | convolution fusion | flops 1610743808 | bytes 5242880 | tf_op jit(solution)/shard_map/dot_general | solution.py:10
  164.2 16.0 %all-gather.8.cloned.1.call-done = f32[2,512,512]{2,1,0:T(8,128)} async-done(((f32[2,64,512]{2,1,0:T(8,128)}), f32[2,512,512]{2,1,0:T(8,128)}) %all-gather.8.cloned.1.call-update) | async-done | bytes 2097168 | tf_op jit(solution)/shard_map/all_gather | solution.py:49
  180.2 3.7 %fusion.12 = f32[2,512,256]{2,1,0:T(8,128)S(1)} fusion(f32[2,512,512]{2,1,0:T(8,128)} %all-gather.8.cloned.1.call-done, f32[2,1,512,256]{3,2,1,0:T(8,128)S(1)} %copy-done), kind=kOutput, calls=%fused_computation.17 | convolution fusion | flops 1610612736 | bytes 4194304 | tf_op jit(solution)/shard_map/dot_general | solution.py:10
  184.0 4.7 %multiply_reduce_fusion.1 = (f32[512,256]{1,0:T(8,128)}, f32[2,512,256]{2,1,0:T(8,128)S(1)}) fusion(f32[2]{0:T(128)S(1)} %copy-done.11, f32[2,512,256]{2,1,0:T(8,128)S(1)} %fusion.12, f32[2,1024,512]{1,2,0:T(8,128)S(1)} %copy-done.1, f32[2,1024,256]{1,2,0:T(8,128)S(1)} %bitcast_multiply_fusion), kind=kOutput, calls=%fused_computation.20 | convolution fusion | flops 3222142976 | bytes 8912904 | tf_op jit(solution)/shard_map/dot_general | solution.py:10
  188.7 2.6 fusion.9
  191.2 68.0 %all-reduce.3.cloned.1.call-done = (f32[16,1024]{1,0:T(8,128)}, f32[1,1024,64]{1,2,0:T(8,128)}, f32[1,64,512]{2,1,0:T(8,128)}, f32[1,1024,256]{1,2,0:T(8,128)}, ...) async-done(((f32[16,1024]{1,0:T(8,128)}, f32[1,1024,64]{1,2,0:T(8,128)}, f32[1,64,512]{2,1,0:T(8,128)}, f32[1,1024,256]{1,2,0:T(8,128)}, f32[1,512,256]{2,1,0:T(8,128)}, ...) | async-done | bytes 2293776 | tf_op jit(solution)/shard_map/psum | solution.py:66
  259.3 2.6 copy.26
  261.9 0.6 copy.38
  262.6 0.7 copy.39
  263.3 0.7 copy.40
  263.9 0.8 copy.41
  264.7 0.7 copy.42
  (33 shorter events, 0.3 us)
Async XLA Ops:
  7.2 146.2 %copy-start = (f32[2,1,512,256]{3,2,1,0:T(8,128)S(1)}, f32[2,1,512,256]{3,2,1,0:T(8,128)}, u32[]{:S(2)}) copy-start(f32[2,1,512,256]{3,2,1,0:T(8,128)} %param.12) | copy-start | bytes 3145732
  7.2 90.8 %all-gather.4.cloned.1.call-start = ((), (), s32[]{:S(2)}) async-start(), calls=%async_computation | async-start | bytes 8519680 | tf_op jit(solution)/shard_map/all_gather | solution.py:36
  7.9 3.0 %copy-start.12 = (s32[1,8]{1,0:T(1,128)S(1)}, s32[1,8]{1,0:T(1,128)}, u32[]{:S(2)}) copy-start(s32[1,8]{1,0:T(1,128)} %param.14) | copy-start | bytes 100
  7.9 136.6 %all-gather.6.cloned.1.call-start = ((), (), s32[]{:S(2)}) async-start(), calls=%async_computation.1 | async-start | bytes 4718592 | tf_op jit(solution)/shard_map/all_gather | solution.py:42
  98.0 12.9 %copy-start.11 = (f32[2]{0:T(128)S(1)}, f32[2]{0:T(128)}, u32[]{:S(2)}) copy-start(f32[2]{0:T(128)} %param.15) | copy-start | bytes 28
  109.4 1.5 copy-start.2
  112.5 67.8 %all-gather.8.cloned.1.call-start = ((), (), s32[]{:S(2)}) async-start(), calls=%async_computation.2 | async-start | bytes 2359296 | tf_op jit(solution)/shard_map/all_gather | solution.py:49
  112.5 40.1 %copy-start.6 = (f32[2,16,1024]{2,1,0:T(8,128)S(1)}, f32[2,16,1024]{2,1,0:T(8,128)}, u32[]{:S(2)}) copy-start(f32[2,16,1024]{2,1,0:T(8,128)} %param.8) | copy-start | bytes 393220
  152.4 106.9 %all-reduce.3.cloned.1.call-start = ((), (), s32[]{:S(2)}) async-start(), calls=%async_computation.3 | async-start | bytes 4587520 | tf_op jit(solution)/shard_map/psum | solution.py:66
  153.3 8.0 %copy-start.4 = (f32[2,1,256,256]{3,2,1,0:T(8,128)S(1)}, f32[2,1,256,256]{3,2,1,0:T(8,128)}, u32[]{:S(2)}) copy-start(f32[2,1,256,256]{3,2,1,0:T(8,128)} %param.13) | copy-start | bytes 1572868
  180.2 3.7 %copy-start.1 = (f32[2,1024,512]{1,2,0:T(8,128)S(1)}, f32[2,1024,512]{1,2,0:T(8,128)}, u32[]{:S(2)}) copy-start(f32[2,1024,512]{1,2,0:T(8,128)} %all-gather.6.cloned.1.call-done) | copy-start | bytes 12582916
  184.0 4.7 %copy-start.3 = (f32[2,256,256]{2,1,0:T(8,128)S(1)}, f32[2,256,256]{2,1,0:T(8,128)}, u32[]{:S(2)}) copy-start(f32[2,256,256]{2,1,0:T(8,128)} %convolution_add_fusion.1) | copy-start | bytes 1572868
  259.3 2.6 copy-start.10
  259.3 3.3 %copy-start.8 = (f32[1,1024,64]{1,2,0:T(8,128)S(1)}, f32[1,1024,64]{1,2,0:T(8,128)}, u32[]{:S(2)}) copy-start(f32[1,1024,64]{1,2,0:T(8,128)} %get-tuple-element.27) | copy-start | bytes 786436
  259.3 4.0 %copy-start.9 = (f32[1,64,512]{2,1,0:T(8,128)S(1)}, f32[1,64,512]{2,1,0:T(8,128)}, u32[]{:S(2)}) copy-start(f32[1,64,512]{2,1,0:T(8,128)} %get-tuple-element.28) | copy-start | bytes 393220
  259.3 4.6 %copy-start.5 = (f32[1,512,256]{2,1,0:T(8,128)S(1)}, f32[1,512,256]{2,1,0:T(8,128)}, u32[]{:S(2)}) copy-start(f32[1,512,256]{2,1,0:T(8,128)} %get-tuple-element.30) | copy-start | bytes 1572868
  259.3 5.4 %copy-start.7 = (f32[1,256,256]{2,1,0:T(8,128)S(1)}, f32[1,256,256]{2,1,0:T(8,128)}, u32[]{:S(2)}) copy-start(f32[1,256,256]{2,1,0:T(8,128)} %get-tuple-element.31) | copy-start | bytes 786436
Sparse Core Ops, SparseCore 0:
  10.8 87.1 all-gather.3
  112.6 31.8 all-gather.5
  152.5 27.6 all-gather.7
  191.4 67.8 all-reduce.2
where the time goes:
time: 272 us
  waiting for transfers between devices  202 us (74%)
  matrix products  41 us (15%)
  between operations  13.9 us (5%)
  local copies, waits for them, and re-layouts  10.7 us (4%)
  other arithmetic  4.09 us (2%)
    all_gather x1, waiting for transfers between devices, shards(): lax.all_gather(root_inverse, ('row', 'col'), axis=1, tiled=True)  85.2 us
    psum x1, waiting for transfers between devices, shards(): lax.psum((upper_levels[0], upper_levels[1], upper_levels[2], leaf_levels[...  68 us
    dot_general x7, matrix products, product(): return jnp.matmul(left, right, precision=highest)  41 us
    all_gather x1, waiting for transfers between devices, shards(): piece = lax.all_gather(offdiag, 'col', axis=2, tiled=True)  31.9 us
    all_gather x1, waiting for transfers between devices, shards(): lax.all_gather(diag_rows, 'col', axis=1, tiled=True)  16 us
    unnamed x33, local copies, waits for them, and re-layouts  10.6 us
  transfers between devices with their start and end apart: 4, of which 4 were waited for; matrix products, arithmetic and copies ran while one was open for 6% of the time, Pallas kernels for 0%

commit v1 on v0

--- a/solution.py
+++ b/solution.py
@@ -39,7 +39,8 @@
     col_index = lax.axis_index("col")
     own_rows = lax.dynamic_slice_in_dim(node_inv, col_index * width, width, 1)
     factor_t = jnp.swapaxes(node_cols, 1, 2)
-    piece = lax.all_gather(offdiag, "col", axis=2, tiled=True)
+    copies = jnp.concatenate([offdiag] * lax.axis_size("col"), axis=2)
+    piece = lax.all_to_all(copies, "col", 2, 2, tiled=True)
     root_sum = root_times
     root_sum = root_sum + product(piece, node_leaf)
     node_part = product(jnp.swapaxes(piece, 1, 2), root_leaf)

time: 272 us -> 302 us (1.11)
  waiting for transfers between devices: 202 us -> 215 us
  local copies, waits for them, and re-layouts: 10.7 us -> 17.4 us
  matrix products: 41 us -> 46.7 us
  starting transfers between devices: 0.34 us -> 4.81 us
    all_to_all x0 -> x1, waiting for transfers between devices: none -> 48.8 us  [shards(): piece = lax.all_to_all(copies, 'col', 2, 2, tiled=True)]
    all_gather x1 -> x0, waiting for transfers between devices: 31.9 us -> none  [shards(): piece = lax.all_gather(offdiag, 'col', axis=2, tiled=True)]
    dot_general x7, matrix products: 41 us -> 46.7 us  [product(): return jnp.matmul(left, right, precision=highest)]
    concatenate x0 -> x1, local copies, waits for them, and re-layouts: none -> 5.21 us  [shards(): copies = jnp.concatenate([offdiag] * lax.axis_size('col'), axis=2)]
    all_to_all x0 -> x1, starting transfers between devices: none -> 4.67 us  [shards(): piece = lax.all_to_all(copies, 'col', 2, 2, tiled=True)]
    all_gather x1, waiting for transfers between devices: 16 us -> 12.6 us  [shards(): lax.all_gather(diag_rows, 'col', axis=1, tiled=True)]
    unnamed x33 -> x27, local copies, waits for them, and re-layouts: 10.6 us -> 12.1 us
where the time goes in v1:
time: 302 us
  waiting for transfers between devices  215 us (71%)
  matrix products  46.7 us (15%)
  local copies, waits for them, and re-layouts  17.4 us (6%)
  between operations  13.9 us (5%)
  starting transfers between devices  4.81 us (2%)
  other arithmetic  3.64 us (1%)
    all_gather x1, waiting for transfers between devices, shards(): lax.all_gather(root_inverse, ('row', 'col'), axis=1, tiled=True)  85.3 us
    psum x1, waiting for transfers between devices, shards(): lax.psum((upper_levels[0], upper_levels[1], upper_levels[2], leaf_levels[...  68 us
    all_to_all x1, waiting for transfers between devices, shards(): piece = lax.all_to_all(copies, 'col', 2, 2, tiled=True)  48.8 us
    dot_general x7, matrix products, product(): return jnp.matmul(left, right, precision=highest)  46.7 us
    all_gather x1, waiting for transfers between devices, shards(): lax.all_gather(diag_rows, 'col', axis=1, tiled=True)  12.6 us
    unnamed x27, local copies, waits for them, and re-layouts  12.1 us
  transfers between devices with their start and end apart: 4, of which 4 were waited for; matrix products, arithmetic and copies ran while one was open for 6% of the time, Pallas kernels for 0%

profile of v1, /device:TPU:1, one launch (start us, length us, event | category | flops | bytes accessed | tf_op | source)
XLA Modules:
  0.0 301.9 jit_solution(15523009197648540016)
XLA Ops:
  7.2 0.7 all-gather.3.cloned.1.call-update
  7.9 2.9 copy.22
  10.9 1.8 bitcast_multiply_fusion
  12.8 85.3 %all-gather.3.cloned.1.call-done = f32[2,1024,1024]{2,1,0:T(8,128)} async-done(((f32[2,16,1024]{2,1,0:T(8,128)}), f32[2,1024,1024]{2,1,0:T(8,128)}) %all-gather.3.cloned.1.call-update) | async-done | bytes 8388624 | tf_op jit(solution)/shard_map/all_gather | solution.py:36
  98.0 11.3 %fusion.10 = f32[2,1024,320]{1,2,0:T(8,128)S(1)} fusion(f32[2,1024,1024]{2,1,0:T(8,128)} %all-gather.3.cloned.1.call-done, f32[2,1024,256]{1,2,0:T(8,128)S(1)} %bitcast_multiply_fusion, f32[2,1024,64]{1,2,0:T(8,128)} %bitcast.51), kind=kOutput, calls=%fused_computation.13 | convolution fusion | flops 8053719040 | bytes 13631488 | tf_op jit(solution)/shard_map/dot_general | solution.py:10
  109.7 1.2 copy-done.1
  110.9 0.8 fusion.38
  111.8 5.2 %copy.23 = f32[2,1024,512]{1,0,2:T(2,128)} copy(f32[2,1024,512]{1,2,0:T(8,128)S(1)} %get-tuple-element.18) | data formatting | bytes 8388608 | tf_op jit(solution)/shard_map/concatenate | solution.py:42
  117.0 4.7 %all-to-all-start = ((f32[2,1024,512]{1,0,2:T(2,128)}), f32[2,1024,512]{1,0,2:T(2,128)}, u32[]{:S(2)}, u32[]{:S(2)}) async-start(f32[2,1024,512]{1,0,2:T(2,128)} %copy.23), calls=%async_computation | async-start | bytes 8388608 | tf_op jit(solution)/shard_map/all_to_all | solution.py:43
  121.7 48.8 %all-to-all-done = f32[2,1024,512]{1,0,2:T(2,128)} async-done(((f32[2,1024,512]{1,0,2:T(2,128)}), f32[2,1024,512]{1,0,2:T(2,128)}, u32[]{:S(2)}, u32[]{:S(2)}) %all-to-all-start) | async-done | bytes 4194336 | tf_op jit(solution)/shard_map/all_to_all | solution.py:43
  170.6 8.9 %multiply_reduce_fusion.3 = (f32[64,512]{1,0:T(8,128)}, f32[2,64,512]{2,1,0:T(8,128)}) fusion(f32[2]{0:T(128)S(1)} %copy-done.8, f32[2,1,1024,64]{2,3,1,0:T(8,128)} %param.9, f32[2,1024,512]{1,0,2:T(2,128)} %all-to-all-done, f32[2,1,512,512]{3,2,1,0:T(8,128)} %param.10, s32[]{:T(128)S(6)} %select_n.3), kind=kOutput, calls=%fused_computation.29 | convolution fusion | flops 805470208 | bytes 5373964 | tf_op jit(solution)/shard_map/dot_general | solution.py:10
  179.6 0.7 multiply_reduce_fusion.4
  180.3 9.1 %multiply_reduce_fusion = (f32[1024,256]{0,1:T(8,128)}, f32[2,1024,256]{1,2,0:T(8,128)S(1)}) fusion(f32[2]{0:T(128)S(1)} %copy-done.8, f32[2,1,512,256]{3,2,1,0:T(8,128)S(1)} %copy-done, f32[2,1024,512]{1,0,2:T(2,128)} %all-to-all-done, f32[2,1024,320]{1,2,0:T(8,128)} %copy-done.1), kind=kOutput, calls=%fused_computation.12 | convolution fusion | flops 3223060480 | bytes 10485768 | tf_op jit(solution)/shard_map/dot_general | solution.py:10
  189.4 2.9 convolution_add_fusion
  192.4 12.6 %all-gather.5.cloned.1.call-done = f32[2,512,512]{2,1,0:T(8,128)} async-done(((f32[2,64,512]{2,1,0:T(8,128)}), f32[2,512,512]{2,1,0:T(8,128)}) %all-gather.5.cloned.1.call-update) | async-done | bytes 2097168 | tf_op jit(solution)/shard_map/all_gather | solution.py:50
  204.9 3.6 %fusion.28 = f32[2,512,256]{2,1,0:T(8,128)S(1)} fusion(f32[2,512,512]{2,1,0:T(8,128)} %all-gather.5.cloned.1.call-done, f32[2,1,512,256]{3,2,1,0:T(8,128)S(1)} %copy-done), kind=kOutput, calls=%fused_computation.23 | convolution fusion | flops 1610612736 | bytes 4194304 | tf_op jit(solution)/shard_map/dot_general | solution.py:10
  208.5 8.3 %multiply_reduce_fusion.1 = (f32[512,256]{1,0:T(8,128)}, f32[2,512,256]{2,1,0:T(8,128)S(1)}) fusion(f32[2]{0:T(128)S(1)} %copy-done.8, f32[2,512,256]{2,1,0:T(8,128)S(1)} %fusion.28, f32[2,1024,256]{1,2,0:T(8,128)S(1)} %bitcast_multiply_fusion, f32[2,1024,512]{1,0,2:T(2,128)} %all-to-all-done), kind=kOutput, calls=%fused_computation.26 | convolution fusion | flops 3222142976 | bytes 8912904 | tf_op jit(solution)/shard_map/dot_general | solution.py:10
  216.8 2.6 fusion.20
  219.4 68.0 %all-reduce.3.cloned.1.call-done = (f32[16,1024]{1,0:T(8,128)}, f32[1,1024,64]{1,2,0:T(8,128)}, f32[1,64,512]{2,1,0:T(8,128)}, f32[1,1024,256]{1,2,0:T(8,128)}, ...) async-done(((f32[16,1024]{1,0:T(8,128)}, f32[1,1024,64]{1,2,0:T(8,128)}, f32[1,64,512]{2,1,0:T(8,128)}, f32[1,1024,256]{1,2,0:T(8,128)}, f32[1,512,256]{2,1,0:T(8,128)}, ...) | async-done | bytes 2293776 | tf_op jit(solution)/shard_map/psum | solution.py:67
  287.4 2.6 copy.32
  290.0 1.5 copy.71
  291.5 1.7 copy.72
  293.8 0.8 copy.74
  294.6 0.7 copy.75
  (34 shorter events, 1.2 us)
Async XLA Ops:
  7.2 173.2 %copy-start = (f32[2,1,512,256]{3,2,1,0:T(8,128)S(1)}, f32[2,1,512,256]{3,2,1,0:T(8,128)}, u32[]{:S(2)}) copy-start(f32[2,1,512,256]{3,2,1,0:T(8,128)} %param.12) | copy-start | bytes 3145732
  7.2 3.7 %copy-start.9 = (s32[1,8]{1,0:T(1,128)S(1)}, s32[1,8]{1,0:T(1,128)}, u32[]{:S(2)}) copy-start(s32[1,8]{1,0:T(1,128)} %param.14) | copy-start | bytes 100
  7.2 90.8 %all-gather.3.cloned.1.call-start = ((), (), s32[]{:S(2)}) async-start(), calls=%async_computation.1 | async-start | bytes 8519680 | tf_op jit(solution)/shard_map/all_gather | solution.py:36
  109.4 1.6 copy-start.1
  109.5 1.5 copy-start.8
  117.0 53.6 %all-to-all-start = ((f32[2,1024,512]{1,0,2:T(2,128)}), f32[2,1024,512]{1,0,2:T(2,128)}, u32[]{:S(2)}, u32[]{:S(2)}) async-start(f32[2,1024,512]{1,0,2:T(2,128)} %copy.23), calls=%async_computation | async-start | bytes 8388608 | tf_op jit(solution)/shard_map/all_to_all | solution.py:43
  121.7 83.3 %all-gather.5.cloned.1.call-start = ((), (), s32[]{:S(2)}) async-start(), calls=%async_computation.2 | async-start | bytes 2359296 | tf_op jit(solution)/shard_map/all_gather | solution.py:50
  121.7 57.9 %copy-start.5 = (f32[2,16,1024]{2,1,0:T(8,128)S(1)}, f32[2,16,1024]{2,1,0:T(8,128)}, u32[]{:S(2)}) copy-start(f32[2,16,1024]{2,1,0:T(8,128)} %param.8) | copy-start | bytes 393220
  179.6 107.9 %all-reduce.3.cloned.1.call-start = ((), (), s32[]{:S(2)}) async-start(), calls=%async_computation.3 | async-start | bytes 4587520 | tf_op jit(solution)/shard_map/psum | solution.py:67
  180.3 9.1 %copy-start.3 = (f32[2,1,256,256]{3,2,1,0:T(8,128)S(1)}, f32[2,1,256,256]{3,2,1,0:T(8,128)}, u32[]{:S(2)}) copy-start(f32[2,1,256,256]{3,2,1,0:T(8,128)} %param.13) | copy-start | bytes 1572868
  208.5 8.3 %copy-start.2 = (f32[2,256,256]{2,1,0:T(8,128)S(1)}, f32[2,256,256]{2,1,0:T(8,128)}, u32[]{:S(2)}) copy-start(f32[2,256,256]{2,1,0:T(8,128)} %convolution_add_fusion) | copy-start | bytes 1572868
  287.4 5.8 %copy-start.7 = (f32[1,64,512]{2,1,0:T(8,128)S(1)}, f32[1,64,512]{2,1,0:T(8,128)}, u32[]{:S(2)}) copy-start(f32[1,64,512]{2,1,0:T(8,128)} %get-tuple-element.28) | copy-start | bytes 393220
  287.4 6.4 %copy-start.4 = (f32[1,512,256]{2,1,0:T(8,128)S(1)}, f32[1,512,256]{2,1,0:T(8,128)}, u32[]{:S(2)}) copy-start(f32[1,512,256]{2,1,0:T(8,128)} %get-tuple-element.30) | copy-start | bytes 1572868
  287.4 7.2 %copy-start.6 = (f32[1,256,256]{2,1,0:T(8,128)S(1)}, f32[1,256,256]{2,1,0:T(8,128)}, u32[]{:S(2)}) copy-start(f32[1,256,256]{2,1,0:T(8,128)} %get-tuple-element.31) | copy-start | bytes 786436
Sparse Core Ops, SparseCore 0:
  10.8 87.1 all-gather.2
  179.7 25.2 all-gather.4
  219.5 67.8 all-reduce.2
